TPU v7x, 32 devices: a whole 2x2x4 slice. The times are simulated.
32 devices in a mesh: clus: 8 (over z, x), pair: 4 (over y, core).
Axes of the slice: x: 2, y: 2, z: 4, core: 2. Of those that a mesh axis runs over, the one named last changes fastest.
Arguments:
- child_basis: float32 [64, 256, 256], P('clus'), as said below
- transfer: float32 [64, 256, 256], P('clus'), may hold values from -0.5 to 0.5
- child_parent: int32 [8, 8], P('clus'), may hold values from 0 to 1, never falling along the last dimension, each value on 1 to 6 neighbouring positions
- upper_weight: float32 [16, 256, 256], P('clus'), as said below
- child_pairs: int32 [384, 2], P(('clus', 'pair')), may hold values from -1 to 63, as said below
- child_blocks: float32 [384, 256, 256], P(('clus', 'pair')), may hold values from -0.15625 to 0.15625
- parent_pairs: int32 [256, 2], P(('clus', 'pair')), may hold values from -1 to 15, as said below
- parent_blocks: float32 [256, 256, 256], P(('clus', 'pair')), may hold values from -0.15625 to 0.15625
Outputs:
- child_weight: float32 [64, 256, 256], P('clus')
- parent_basis: float32 [16, 256, 256], P('clus')
Inputs may be any that keep to these rules, and one draw needn't show every extreme that they name: `child_pairs`: each device's aligned block of 12 rows holds its valid pairs first and then rows of -1, -1; every block has one valid row or more and some block is full. In the block of flat device index d (clus index c = d // 4), box i lies among the 8 boxes of clus index c, box j among those of clus indices c to c + 3, and j differs from i. `parent_pairs`: as for child_pairs, with blocks of 8 rows and the 2 parent boxes of each clus index. `child_basis`: symmetric positive definite. `upper_weight`: symmetric positive definite.
All inputs are finite; a program needn't handle non-finite values.
Results may differ from a plain program's by a relative error of at most 0.0003.
Values sent between devices are 32-bit elements; how exact they have to be, the bound alone decides.
A program may use at most 128 MiB of HBM per device.

v0:
```python
import jax
import jax.numpy as jnp
from jax import lax
from jax.sharding import PartitionSpec as P

REACH = 3


HIGHEST = lax.Precision.HIGHEST


def shifted(value, axis, steps):
    count = lax.axis_size(axis)
    first, last = (max(0, -steps), min(count, count - steps))
    return lax.ppermute(value, axis, [(source, source + steps) for source in range(first, last)])


def pair_terms(pair_list, blocks, gram_set, window, first_box):
    usable = pair_list[:, 0] >= 0
    near_local = jnp.where(usable, pair_list[:, 0] - first_box, 0)
    far_local = jnp.where(usable, pair_list[:, 1] - first_box, 0)
    near_gram = jnp.take(gram_set, near_local, axis=0)
    far_gram = jnp.take(window, far_local, axis=0)
    near_term = jnp.einsum("pab,pbc->pac", blocks, far_gram, precision=HIGHEST)
    near_term = jnp.einsum("pac,pdc->pad", near_term, blocks, precision=HIGHEST)
    far_term = jnp.einsum("pba,pbc->pac", blocks, near_gram, precision=HIGHEST)
    far_term = jnp.einsum("pac,pcd->pad", far_term, blocks, precision=HIGHEST)
    box_count = gram_set.shape[0]
    slot_count = window.shape[0]
    extent = gram_set.shape[-1]
    near_hot = ((jnp.arange(box_count)[:, None] == near_local[None, :]) & usable[None, :]).astype(
        jnp.float32
    )
    far_hot = ((jnp.arange(slot_count)[:, None] == far_local[None, :]) & usable[None, :]).astype(
        jnp.float32
    )
    near_sum = jnp.einsum("bp,pkl->bkl", near_hot, near_term, precision=HIGHEST)
    far_sum = jnp.einsum("sp,pkl->skl", far_hot, far_term, precision=HIGHEST)
    return (near_sum, far_sum.reshape(slot_count // box_count, box_count, extent, extent))


def lower_weights(transfer, parent_weight, parent_hot):
    chosen = jnp.einsum("pc,pab->cab", parent_hot, parent_weight, precision=HIGHEST)
    lowered = jnp.einsum("cab,cbd->cad", transfer, chosen, precision=HIGHEST)
    return jnp.einsum("cad,ced->cae", lowered, transfer, precision=HIGHEST)


def per_device(
    child_basis,
    transfer,
    child_parent,
    upper_weight,
    child_pairs,
    child_blocks,
    parent_pairs,
    parent_blocks,
):
    box_count = child_basis.shape[0]
    parent_count = upper_weight.shape[0]
    clus_index = lax.axis_index("clus")
    parent_hot = (jnp.arange(parent_count)[:, None] == child_parent[0][None, :]).astype(jnp.float32)
    lifted = jnp.einsum("cba,cbd->cad", transfer, child_basis, precision=HIGHEST)
    lifted = jnp.einsum("cad,cde->cae", lifted, transfer, precision=HIGHEST)
    parent_basis = jnp.einsum("pc,cab->pab", parent_hot, lifted, precision=HIGHEST)
    parent_pieces = [parent_basis]
    for offset in range(1, REACH + 1):
        parent_pieces.append(shifted(parent_basis, "clus", -offset))
    parent_window = jnp.concatenate(parent_pieces, axis=0)
    parent_near, parent_far = pair_terms(
        parent_pairs, parent_blocks, parent_basis, parent_window, clus_index * parent_count
    )
    parent_partial = parent_near + parent_far[0]
    for offset in range(1, REACH + 1):
        parent_partial = parent_partial + shifted(parent_far[offset], "clus", offset)
    mixed = parent_partial + upper_weight * (1.0 / lax.axis_size("pair"))
    local_extra = lower_weights(transfer, mixed, parent_hot)
    child_first = clus_index * box_count
    pieces = [child_basis]
    for offset in range(1, REACH + 1):
        pieces.append(shifted(child_basis, "clus", -offset))
    window = jnp.concatenate(pieces, axis=0)
    child_near, child_far = pair_terms(child_pairs, child_blocks, child_basis, window, child_first)
    partial_value = child_near + child_far[0] + local_extra
    for offset in range(1, REACH + 1):
        partial_value = partial_value + shifted(child_far[offset], "clus", offset)
    child_weight = lax.psum(partial_value, "pair")
    return (child_weight, parent_basis)


def solution(mesh):
    return jax.shard_map(
        per_device,
        mesh=mesh,
        in_specs=(
            P("clus", None, None),
            P("clus", None, None),
            P("clus", None),
            P("clus", None, None),
            P(("clus", "pair"), None),
            P(("clus", "pair"), None, None),
            P(("clus", "pair"), None),
            P(("clus", "pair"), None, None),
        ),
        out_specs=(P("clus", None, None), P("clus", None, None)),
        check_vma=False,
    )
```

profile of v0, /device:TPU:0, one launch (start us, length us, event | category | flops | bytes accessed | tf_op | source)
XLA Modules:
  0.0 403.6 jit_solution(8069345369113619741)
XLA Ops:
  7.2 0.0 copy-start
  7.2 0.0 all-reduce.2.cloned.1.call-start
  7.2 0.0 copy-start.3
  7.2 5.9 %fusion.85 = f32[8,256,256]{2,1,0:T(8,128)S(1)} fusion(f32[8,256,256]{2,1,0:T(8,128)} %param.9, f32[8,256,256]{2,1,0:T(8,128)} %param.8), kind=kOutput, calls=%fused_computation.102 | convolution fusion | flops 1610612736 | bytes 6291456 | tf_op jit(solution)/shard_map/cba,cbd->cad/dot_general | solution.py:62
  13.1 0.0 copy-start.12
  13.1 2.2 fusion.86
  15.3 0.0 copy-start.10
  15.3 3.0 fusion.18
  18.3 1.3 collective-permute-start.5
  19.6 1.3 collective-permute-start.4
  20.9 1.3 collective-permute-start.3
  22.2 1.6 collective-permute-start.2
  23.9 1.9 copy.15
  25.8 3.0 gather_fusion.3
  28.8 6.0 %fusion.20 = f32[8,256,256]{2,1,0:T(8,128)S(1)} fusion(f32[8,256,256]{2,1,0:T(8,128)} %param.15, f32[8,256,256]{2,1,0:T(8,128)} %gather_fusion.3, pred[8]{0:T(512)(128)(4,1)S(1)} %get-tuple-element.28), kind=kOutput, calls=%fused_computation.27 | convolution fusion | flops 1611137024 | bytes 6291464 | tf_op jit(solution)/shard_map/pba,pbc->pac/dot_general | solution.py:26
  34.8 3.6 fusion.88
  38.4 2.2 fusion.14
  40.6 1.4 copy-done.6
  42.0 1.6 fusion.82
  43.6 6.8 %collective-permute-start.6 = (f32[2,256,256]{2,0,1:T(2,128)}, f32[2,256,256]{2,0,1:T(2,128)}, u32[]{:S(2)}, u32[]{:S(2)}) collective-permute-start(f32[2,256,256]{2,0,1:T(2,128)} %get-tuple-element.17), channel_id=1, source_target_pairs={{0,4},{4,8},{8,12},{12,16},{16,20},{20,24},{24,28},{1,5},{5,9},{9,... | collective-permute-start | bytes 1572872 | tf_op jit(solution)/shard_map/ppermute | solution.py:15
  50.5 4.0 gather_fusion.1
  54.5 7.2 %fusion.4 = f32[12,256,256]{2,1,0:T(8,128)S(1)} fusion(f32[12,256,256]{2,1,0:T(8,128)S(1)} %copy-done, f32[12,256,256]{2,1,0:T(8,128)} %gather_fusion.1, pred[12]{0:T(512)(128)(4,1)S(1)} %get-tuple-element.23), kind=kOutput, calls=%fused_computation.9 | convolution fusion | flops 2416705536 | bytes 9437196 | tf_op jit(solution)/shard_map/pba,pbc->pac/dot_general | solution.py:26
  61.7 5.1 %fusion.84 = f32[12,256,256]{2,1,0:T(8,128)S(1)} fusion(f32[12,256,256]{2,1,0:T(8,128)S(1)} %fusion.4, f32[12,256,256]{2,1,0:T(8,128)S(1)} %copy-done), kind=kOutput, calls=%fused_computation.101 | convolution fusion | flops 2415919104 | bytes 9437184 | tf_op jit(solution)/shard_map/pac,pcd->pad/dot_general | solution.py:27
  66.8 5.3 %fusion = f32[32,256,256]{2,0,1:T(8,128)S(1)} fusion(f32[12,256,256]{2,1,0:T(8,128)S(1)} %fusion.84, s32[12]{0:T(128)S(1)} %get-tuple-element.21, pred[12]{0:T(512)(128)(4,1)S(1)} %get-tuple-element.22), kind=kOutput, calls=%fused_computation.5 | convolution fusion | flops 301990656 | bytes 11534396 | tf_op jit(solution)/shard_map/sp,pkl->skl/dot_general | solution.py:38
  72.1 3.1 fusion.81
  75.2 2.1 copy-done.5
  77.3 0.0 collective-permute-done.5
  77.4 1.3 collective-permute-start.1
  78.6 0.0 collective-permute-done.4
  78.7 1.3 collective-permute-start
  80.0 0.0 collective-permute-done.3
  80.0 41.5 %collective-permute-start.8 = (f32[2,256,256]{2,0,1:T(2,128)}, f32[2,256,256]{2,0,1:T(2,128)}, u32[]{:S(2)}, u32[]{:S(2)}) collective-permute-start(f32[2,256,256]{2,0,1:T(2,128)} %get-tuple-element.18), channel_id=1, source_target_pairs={{0,12},{4,16},{8,20},{12,24},{16,28},{1,13},{5,17},{9,21},{13,25},... | collective-permute-start | bytes 1572872 | tf_op jit(solution)/shard_map/ppermute | solution.py:15
  121.5 2.5 pad_maximum_fusion.1
  123.9 1.9 copy.14
  125.9 3.6 gather_fusion.2
  129.5 0.0 collective-permute-done.6
  129.5 1.5 collective-permute-start.7
  131.0 0.0 copy-start.2
  131.1 6.0 %fusion.22 = f32[8,256,256]{2,1,0:T(8,128)S(1)} fusion(f32[8,256,256]{2,1,0:T(8,128)} %param.15, f32[8,256,256]{2,1,0:T(8,128)} %gather_fusion.2, pred[8]{0:T(512)(128)(4,1)S(1)} %get-tuple-element.8), kind=kOutput, calls=%fused_computation.29 | convolution fusion | flops 1611137024 | bytes 6291464 | tf_op jit(solution)/shard_map/pab,pbc->pac/dot_general | solution.py:24
  137.1 0.0 copy-start.9
  137.1 3.6 fusion.87
  140.7 0.0 collective-permute-done.8
  140.7 3.7 collective-permute-start.9
  144.4 0.0 collective-permute-done.7
  144.4 12.2 %collective-permute-start.11 = (f32[8,256,256]{2,0,1:T(8,128)}, f32[8,256,256]{2,0,1:T(8,128)}, u32[]{:S(2)}, u32[]{:S(2)}) collective-permute-start(f32[8,256,256]{2,0,1:T(8,128)} %get-tuple-element.15), channel_id=1, source_target_pairs={{0,12},{4,16},{8,20},{12,24},{16,28},{1,13},{5,17},{9,21},{13,25},... | collective-permute-start | bytes 6291464 | tf_op jit(solution)/shard_map/ppermute | solution.py:15
  156.5 4.2 %fusion.42 = f32[2,256,256]{2,0,1:T(2,128)S(1)} fusion(f32[2,256,256]{2,0,1:T(2,128)} %collective-permute-done.8, f32[2,256,256]{2,0,1:T(2,128)S(1)} %collective-permute-done.7, f32[2,256,256]{2,0,1:T(2,128)} %collective-permute-done.6, f32[8,256,256]{2,1,0:T(8,128)S(1)} %fusion.87, f32[8,256,256]{2,0,1:T(8,128)S(1)} %copy-done.7, ...), kind=kOutput, calls=%fused_computation.39 | convolution fusion | flops 13369376 | bytes 5242920 | tf_op jit(solution)/shard_map/bp,pkl->bkl/dot_general | solution.py:37
  160.8 0.0 copy-start.4
  160.8 0.0 collective-permute-done.2
  160.8 5.9 %collective-permute-start.10 = (f32[8,256,256]{2,0,1:T(8,128)}, f32[8,256,256]{2,0,1:T(8,128)}, u32[]{:S(2)}, u32[]{:S(2)}) collective-permute-start(f32[8,256,256]{2,0,1:T(8,128)} %get-tuple-element.16), channel_id=1, source_target_pairs={{0,8},{4,12},{8,16},{12,20},{16,24},{20,28},{1,9},{5,13},{9,17},{1... | collective-permute-start | bytes 6291464 | tf_op jit(solution)/shard_map/ppermute | solution.py:15
  166.7 1.3 fusion.63
  168.1 2.9 fusion.12
  171.0 3.4 fusion.89
  174.4 0.0 collective-permute-done.1
  174.4 6.3 %pad_maximum_fusion = f32[32,256,256]{2,1,0:T(8,128)} fusion(f32[8,256,256]{2,1,0:T(8,128)} %collective-permute-done.2, f32[8,256,256]{2,1,0:T(8,128)} %collective-permute-done.1, f32[8,256,256]{2,1,0:T(8,128)} %collective-permute-done, f32[8,256,256]{2,1,0:T(8,128)} %param.8), kind=kLoop, calls=%fused_computation.4 | loop fusion | flops 6291456 | bytes 16777216 | tf_op jit(solution)/shard_map/concatenate | solution.py:81
  180.7 5.8 %gather_fusion = f32[12,256,256]{2,1,0:T(8,128)} fusion(f32[32,256,256]{2,1,0:T(8,128)} %pad_maximum_fusion, s32[1024]{0:T(1024)S(1)} %pad_clamp_fusion.3), kind=kCustom, calls=%fused_computation | custom fusion | bytes 6291504 | tf_op jit(solution)/shard_map/jit(_take)/gather | solution.py:23
  186.5 7.3 %fusion.6 = f32[12,256,256]{2,1,0:T(8,128)S(1)} fusion(f32[12,256,256]{2,1,0:T(8,128)S(1)} %copy-done, f32[12,256,256]{2,1,0:T(8,128)} %gather_fusion, pred[12]{0:T(512)(128)(4,1)S(1)} %get-tuple-element.6), kind=kOutput, calls=%fused_computation.11 | convolution fusion | flops 2416705536 | bytes 9437196 | tf_op jit(solution)/shard_map/pab,pbc->pac/dot_general | solution.py:24
  193.8 5.4 %fusion.83 = f32[12,256,256]{2,1,0:T(8,128)S(1)} fusion(f32[12,256,256]{2,1,0:T(8,128)S(1)} %fusion.6, f32[12,256,256]{2,1,0:T(8,128)S(1)} %copy-done), kind=kOutput, calls=%fused_computation.100 | convolution fusion | flops 2415919104 | bytes 9437184 | tf_op jit(solution)/shard_map/pac,pdc->pad/dot_general | solution.py:25
  199.2 51.0 %collective-permute-done.9 = f32[8,256,256]{2,0,1:T(8,128)} collective-permute-done((f32[8,256,256]{2,0,1:T(8,128)}, f32[8,256,256]{2,0,1:T(8,128)}, u32[]{:S(2)}, u32[]{:S(2)}) %collective-permute-start.9) | collective-permute-done | bytes 2097184 | tf_op jit(solution)/shard_map/ppermute | solution.py:15
  250.1 0.0 collective-permute-done.11
  250.2 0.0 collective-permute-done.10
  250.2 10.0 %fusion.11 = f32[8,256,256]{2,0,1:T(8,128)} fusion(f32[8,256,256]{2,0,1:T(8,128)} %collective-permute-done.11, f32[8,256,256]{2,0,1:T(8,128)} %collective-permute-done.10, f32[8,256,256]{2,0,1:T(8,128)} %collective-permute-done.9, f32[32,256,256]{2,0,1:T(8,128)} %copy-done.5, f32[8,256,256]{2,1,0:T(8,128)S(1)} %copy-done.8, ...), kind=kOutput, calls=%fused_computation.17 | convolution fusion | flops 78119104 | bytes 15728700 | tf_op jit(solution)/shard_map/bp,pkl->bkl/dot_general | solution.py:37
  260.1 0.0 all-reduce.2.cloned.1.call-update
  260.1 132.9 %all-reduce.2.cloned.1.call-done = f32[8,256,256]{2,0,1:T(8,128)} async-done(((f32[8,256,256]{2,0,1:T(8,128)}), f32[8,256,256]{2,0,1:T(8,128)}) %all-reduce.2.cloned.1.call-update) | async-done | bytes 2097168 | tf_op jit(solution)/shard_map/psum | solution.py:86
  393.0 3.6 copy.18
  (26 shorter events, 0.1 us)
Async XLA Ops:
  7.2 47.3 %copy-start = (f32[12,256,256]{2,1,0:T(8,128)S(1)}, f32[12,256,256]{2,1,0:T(8,128)}, u32[]{:S(2)}) copy-start(f32[12,256,256]{2,1,0:T(8,128)} %param.13) | copy-start | bytes 9437188
  7.2 385.8 %all-reduce.2.cloned.1.call-start = ((), (), s32[]{:S(2)}) async-start(), calls=%async_computation | async-start | bytes 4194304 | tf_op jit(solution)/shard_map/psum | solution.py:86
  7.2 5.9 %copy-start.3 = (f32[8,256,256]{2,1,0:T(8,128)S(1)}, f32[8,256,256]{2,1,0:T(8,128)}, u32[]{:S(2)}) copy-start(f32[8,256,256]{2,1,0:T(8,128)} %param.9) | copy-start | bytes 6291460
  13.1 2.2 copy-start.12
  15.3 8.5 %copy-start.10 = (s32[8,2]{0,1:T(2,128)S(1)}, s32[8,2]{0,1:T(2,128)}, u32[]{:S(2)}) copy-start(s32[8,2]{0,1:T(2,128)} %param.14) | copy-start | bytes 196
  18.3 59.0 %collective-permute-start.5 = (f32[2,256,256]{2,0,1:T(2,128)}, f32[2,256,256]{2,0,1:T(2,128)}, u32[]{:S(2)}, u32[]{:S(2)}) collective-permute-start(f32[2,256,256]{2,0,1:T(2,128)} %fusion.18), channel_id=1, source_target_pairs={{12,0},{16,4},{20,8},{24,12},{28,16},{13,1},{17,5},{21,9},{25,13},... | collective-permute-start | bytes 1572872 | tf_op jit(solution)/shard_map/ppermute | solution.py:15
  19.6 59.0 %collective-permute-start.4 = (f32[2,256,256]{2,0,1:T(2,128)}, f32[2,256,256]{2,0,1:T(2,128)}, u32[]{:S(2)}, u32[]{:S(2)}) collective-permute-start(f32[2,256,256]{2,0,1:T(2,128)} %fusion.18), channel_id=1, source_target_pairs={{8,0},{12,4},{16,8},{20,12},{24,16},{28,20},{9,1},{13,5},{17,9},{2... | collective-permute-start | bytes 1572872 | tf_op jit(solution)/shard_map/ppermute | solution.py:15
  20.9 59.0 %collective-permute-start.3 = (f32[2,256,256]{2,0,1:T(2,128)}, f32[2,256,256]{2,0,1:T(2,128)}, u32[]{:S(2)}, u32[]{:S(2)}) collective-permute-start(f32[2,256,256]{2,0,1:T(2,128)} %fusion.18), channel_id=1, source_target_pairs={{4,0},{8,4},{12,8},{16,12},{20,16},{24,20},{28,24},{5,1},{9,5},{13... | collective-permute-start | bytes 1572872 | tf_op jit(solution)/shard_map/ppermute | solution.py:15
  22.2 138.6 %collective-permute-start.2 = (f32[8,256,256]{2,1,0:T(8,128)}, f32[8,256,256]{2,1,0:T(8,128)}, u32[]{:S(2)}, u32[]{:S(2)}) collective-permute-start(f32[8,256,256]{2,1,0:T(8,128)} %param.8), channel_id=1, source_target_pairs={{12,0},{16,4},{20,8},{24,12},{28,16},{13,1},{17,5},{21,9},{25,13},... | collective-permute-start | bytes 6291464 | tf_op jit(solution)/shard_map/ppermute | solution.py:15
  28.8 6.0 %copy-start.1 = (f32[8,256,256]{2,1,0:T(8,128)S(1)}, f32[8,256,256]{2,1,0:T(8,128)}, u32[]{:S(2)}) copy-start(f32[8,256,256]{2,1,0:T(8,128)} %param.15) | copy-start | bytes 6291460
  40.6 1.4 copy-start.6
  42.0 8.4 %copy-start.11 = (s32[12,2]{0,1:T(2,128)S(1)}, s32[12,2]{0,1:T(2,128)}, u32[]{:S(2)}) copy-start(s32[12,2]{0,1:T(2,128)} %param.12) | copy-start | bytes 292
  43.6 85.9 %collective-permute-start.6 = (f32[2,256,256]{2,0,1:T(2,128)}, f32[2,256,256]{2,0,1:T(2,128)}, u32[]{:S(2)}, u32[]{:S(2)}) collective-permute-start(f32[2,256,256]{2,0,1:T(2,128)} %get-tuple-element.17), channel_id=1, source_target_pairs={{0,4},{4,8},{8,12},{12,16},{16,20},{20,24},{24,28},{1,5},{5,9},{9,... | collective-permute-start | bytes 1572872 | tf_op jit(solution)/shard_map/ppermute | solution.py:15
  72.1 5.3 %copy-start.5 = (f32[32,256,256]{2,0,1:T(8,128)}, f32[32,256,256]{2,0,1:T(8,128)S(1)}, u32[]{:S(2)}) copy-start(f32[32,256,256]{2,0,1:T(8,128)S(1)} %fusion) | copy-start | bytes 25165828
  77.4 97.1 %collective-permute-start.1 = (f32[8,256,256]{2,1,0:T(8,128)}, f32[8,256,256]{2,1,0:T(8,128)}, u32[]{:S(2)}, u32[]{:S(2)}) collective-permute-start(f32[8,256,256]{2,1,0:T(8,128)} %param.8), channel_id=1, source_target_pairs={{8,0},{12,4},{16,8},{20,12},{24,16},{28,20},{9,1},{13,5},{17,9},{2... | collective-permute-start | bytes 6291464 | tf_op jit(solution)/shard_map/ppermute | solution.py:15
  78.7 95.8 %collective-permute-start = (f32[8,256,256]{2,1,0:T(8,128)}, f32[8,256,256]{2,1,0:T(8,128)}, u32[]{:S(2)}, u32[]{:S(2)}) collective-permute-start(f32[8,256,256]{2,1,0:T(8,128)} %param.8), channel_id=1, source_target_pairs={{4,0},{8,4},{12,8},{16,12},{20,16},{24,20},{28,24},{5,1},{9,5},{13... | collective-permute-start | bytes 6291464 | tf_op jit(solution)/shard_map/ppermute | solution.py:15
  80.0 60.7 %collective-permute-start.8 = (f32[2,256,256]{2,0,1:T(2,128)}, f32[2,256,256]{2,0,1:T(2,128)}, u32[]{:S(2)}, u32[]{:S(2)}) collective-permute-start(f32[2,256,256]{2,0,1:T(2,128)} %get-tuple-element.18), channel_id=1, source_target_pairs={{0,12},{4,16},{8,20},{12,24},{16,28},{1,13},{5,17},{9,21},{13,25},... | collective-permute-start | bytes 1572872 | tf_op jit(solution)/shard_map/ppermute | solution.py:15
  129.5 14.9 %collective-permute-start.7 = (f32[2,256,256]{2,0,1:T(2,128)}, f32[2,256,256]{2,0,1:T(2,128)S(1)}, u32[]{:S(2)}, u32[]{:S(2)}) collective-permute-start(f32[2,256,256]{2,0,1:T(2,128)} %get-tuple-element.19), channel_id=1, source_target_pairs={{0,8},{4,12},{8,16},{12,20},{16,24},{20,28},{1,9},{5,13},{9,17},{1... | collective-permute-start | bytes 1572872 | tf_op jit(solution)/shard_map/ppermute | solution.py:15
  131.0 6.0 %copy-start.2 = (f32[8,256,256]{2,1,0:T(8,128)S(1)}, f32[8,256,256]{2,1,0:T(8,128)}, u32[]{:S(2)}) copy-start(f32[8,256,256]{2,1,0:T(8,128)} %param.15) | copy-start | bytes 6291460
  137.1 19.5 %copy-start.7 = (f32[8,256,256]{2,0,1:T(8,128)S(1)}, f32[8,256,256]{2,0,1:T(8,128)}, u32[]{:S(2)}) copy-start(f32[8,256,256]{2,0,1:T(8,128)} %copy-done.6) | copy-start | bytes 6291460
  137.1 19.5 %copy-start.9 = (f32[2,256,256]{2,1,0:T(8,128)S(1)}, f32[2,256,256]{2,1,0:T(8,128)}, u32[]{:S(2)}) copy-start(f32[2,256,256]{2,1,0:T(8,128)} %param.11) | copy-start | bytes 1572868
  140.7 109.5 %collective-permute-start.9 = (f32[8,256,256]{2,0,1:T(8,128)}, f32[8,256,256]{2,0,1:T(8,128)}, u32[]{:S(2)}, u32[]{:S(2)}) collective-permute-start(f32[8,256,256]{2,0,1:T(8,128)} %get-tuple-element.14), channel_id=1, source_target_pairs={{0,4},{4,8},{8,12},{12,16},{16,20},{20,24},{24,28},{1,5},{5,9},{9,... | collective-permute-start | bytes 6291464 | tf_op jit(solution)/shard_map/ppermute | solution.py:15
  144.4 105.8 %collective-permute-start.11 = (f32[8,256,256]{2,0,1:T(8,128)}, f32[8,256,256]{2,0,1:T(8,128)}, u32[]{:S(2)}, u32[]{:S(2)}) collective-permute-start(f32[8,256,256]{2,0,1:T(8,128)} %get-tuple-element.15), channel_id=1, source_target_pairs={{0,12},{4,16},{8,20},{12,24},{16,28},{1,13},{5,17},{9,21},{13,25},... | collective-permute-start | bytes 6291464 | tf_op jit(solution)/shard_map/ppermute | solution.py:15
  160.8 7.3 %copy-start.4 = (f32[8,256,256]{2,1,0:T(8,128)S(1)}, f32[8,256,256]{2,1,0:T(8,128)}, u32[]{:S(2)}) copy-start(f32[8,256,256]{2,1,0:T(8,128)} %param.9) | copy-start | bytes 6291460
  160.8 89.4 %collective-permute-start.10 = (f32[8,256,256]{2,0,1:T(8,128)}, f32[8,256,256]{2,0,1:T(8,128)}, u32[]{:S(2)}, u32[]{:S(2)}) collective-permute-start(f32[8,256,256]{2,0,1:T(8,128)} %get-tuple-element.16), channel_id=1, source_target_pairs={{0,8},{4,12},{8,16},{12,20},{16,24},{20,28},{1,9},{5,13},{9,17},{1... | collective-permute-start | bytes 6291464 | tf_op jit(solution)/shard_map/ppermute | solution.py:15
  193.8 56.3 %copy-start.8 = (f32[8,256,256]{2,1,0:T(8,128)S(1)}, f32[8,256,256]{2,1,0:T(8,128)}, u32[]{:S(2)}) copy-start(f32[8,256,256]{2,1,0:T(8,128)} %fusion.89) | copy-start | bytes 6291460
Sparse Core Ops, SparseCore 0:
  260.3 132.7 all-reduce.1
where the time goes:
time: 411 us; the launch traced here: 404 us
  waiting for transfers between devices  184 us (45%)
  matrix products  84.5 us (21%)
  starting transfers between devices  79.7 us (19%)
  local copies, waits for them, and re-layouts  32.1 us (8%)
  between operations  14.7 us (4%)
  other arithmetic  8.83 us (2%)
    psum x1, waiting for transfers between devices, per_device(): child_weight = lax.psum(partial_value, 'pair')  133 us
    ppermute x12, starting transfers between devices, shifted(): lax.ppermute(value, axis, [(source, source + steps) for source in range(f...  79.7 us
    ppermute x12, waiting for transfers between devices, shifted(): lax.ppermute(value, axis, [(source, source + steps) for source in range(f...  51 us
    dot_general x2, matrix products, pair_terms(): near_sum = jnp.einsum('bp,pkl->bkl', near_hot, near_term, precision=HIGHEST)  14.2 us
    dot_general x2, matrix products, pair_terms(): near_term = jnp.einsum('pab,pbc->pac', blocks, far_gram, precision=HIGHEST)  13.3 us
    dot_general x2, matrix products, pair_terms(): far_term = jnp.einsum('pba,pbc->pac', blocks, near_gram, precision=HIGHEST)  13.2 us
    gather x2, local copies, waits for them, and re-layouts, pair_terms(): far_gram = jnp.take(window, far_local, axis=0)  9.39 us
    dot_general x2, matrix products, pair_terms(): near_term = jnp.einsum('pac,pdc->pad', near_term, blocks, precision=HIGHEST)  8.93 us
  transfers between devices with their start and end apart: 13, of which 2 were waited for; matrix products, arithmetic and copies ran while one was open for 24% of the time, Pallas kernels for 0%

commit v1 on v0

v1 whole, which is shorter than its diff:
```python
import functools

import jax
import jax.numpy as jnp
from jax import lax
from jax.experimental import pallas as pl
from jax.experimental.pallas import tpu as pltpu
from jax.sharding import PartitionSpec as P

REACH = 3
CORES = 2
MESH = pl.DeviceIdType.MESH
F32 = jnp.float32
VMEM = pl.BlockSpec(memory_space=pltpu.VMEM)
SMEM = pl.BlockSpec(memory_space=pltpu.SMEM)


def split(x):
    hi = x.astype(jnp.bfloat16)
    return hi, (x - hi.astype(F32)).astype(jnp.bfloat16)


def product(a, b, dims):
    (ah, al), (bh, bl) = a, b
    dot = functools.partial(
        lax.dot_general, dimension_numbers=(dims, ((), ())), preferred_element_type=F32
    )
    return dot(ah, bh) + (dot(ah, bl) + dot(al, bh))


NN = ((1,), (0,))
NT = ((1,), (1,))
TN = ((0,), (0,))


def pack(x):
    h, q = x.shape[0] // 2, x.shape[0] // 4
    low = jnp.concatenate([x[h : h + q, h:], x[h + q :, h:]], axis=1)
    return jnp.concatenate([x[:h], low], axis=0)


def unpack(p):
    n = p.shape[1]
    h, q = n // 2, n // 4
    top = p[:h]
    corner = jnp.concatenate([p[h:, :h], p[h:, h:]], axis=0)
    low = jnp.concatenate([top[:, h:].T, corner], axis=1)
    return jnp.concatenate([top, low], axis=0)


def loop(count, body):
    lax.fori_loop(0, count, lambda i, c: (body(i), c)[1], 0)


def outer_product(s, g):
    s, g = split(s), split(g)
    return product(split(product(s, g, NN)), s, NT)


def inner_product(s, g):
    s, g = split(s), split(g)
    return product(s, split(product(g, s, NN)), TN)


def far_kernel(
    boxes, parents,
    basis, transfer, child_parent, cpairs, cblocks, ppairs, pblocks,
    pbasis, basis_p, pbasis_p, far, pfar,
):
    clus = lax.axis_index("clus")
    pbasis[...] = jnp.zeros_like(pbasis)
    far[...] = jnp.zeros_like(far)
    pfar[...] = jnp.zeros_like(pfar)

    def lift(c):
        g = basis[c]
        basis_p[c] = pack(g)
        p = child_parent[0, c]
        pbasis[p] += inner_product(transfer[c], g)

    loop(boxes, lift)

    def terms(pairs, blocks, grams, sums, count):
        def one(r):
            i, j = pairs[r, 0], pairs[r, 1]

            @pl.when(i >= 0)
            def _():
                t = inner_product(blocks[r], grams[i - clus * count])
                sums[j - clus * count] += pack(t)

        loop(blocks.shape[0], one)

    for p in range(parents):
        pbasis_p[p] = pack(pbasis[p])
    terms(ppairs, pblocks, pbasis, pfar, parents)
    terms(cpairs, cblocks, basis, far, boxes)


def near_kernel(
    boxes, parents, scale,
    cpairs, cblocks, win, ppairs, pblocks, pwin, upper,
    near, pnear,
):
    clus = lax.axis_index("clus")
    near[...] = jnp.zeros_like(near)
    for p in range(parents):
        pnear[p] = pack(upper[p]) * scale

    def terms(pairs, blocks, grams, sums, count):
        def one(r):
            i, j = pairs[r, 0], pairs[r, 1]

            @pl.when(i >= 0)
            def _():
                t = outer_product(blocks[r], unpack(grams[j - clus * count]))
                sums[i - clus * count] += pack(t)

        loop(blocks.shape[0], one)

    terms(ppairs, pblocks, pwin, pnear, parents)
    terms(cpairs, cblocks, win, near, boxes)


def remote(src, dst, sems, index, device):
    send, recv = sems
    return pltpu.make_async_remote_copy(
        src_ref=src, dst_ref=dst, send_sem=send.at[index], recv_sem=recv.at[index],
        device_id=device, device_id_type=MESH,
    )


def place():
    clus, n = lax.axis_index("clus"), lax.axis_size("clus")
    pair = lax.axis_index("pair")
    rows = lax.axis_size("pair") // CORES
    return clus, n, pair // CORES, rows, pair % CORES


def at_pair(clus, y, k):
    return (clus, y * CORES + k)


def meet(clus, n, y, rows, k, along):
    barrier = pltpu.get_barrier_semaphore()

    def tell(device):
        pl.semaphore_signal(barrier, inc=1, device_id=device, device_id_type=MESH)

    tell(at_pair(clus, y, 1 - k))
    for d in range(1, rows):
        tell(at_pair(clus, (y + d) % rows, k))
    peers = rows
    if along:
        for o in range(1, REACH + 1):
            for ok, other in ((clus >= o, clus - o), (clus + o < n, clus + o)):
                @pl.when(ok)
                def _():
                    tell(at_pair(other, y, k))
                peers = peers + ok.astype(jnp.int32)
    pl.semaphore_wait(barrier, peers)


def exchange_kernel(
    boxes, parents,
    basis_p, pbasis_p, far, pfar,
    win, pwin, own, pown,
    half_in, phalf_in, half, phalf, row_in, mine, up_in, pup_in,
    down_s, down_r, pdown_s, pdown_r, core_s, core_r, pcore_s, pcore_r,
    row_s, row_r, up_s, up_r, pup_s, pup_r, fwd_s, fwd_r, pfwd_s, pfwd_r, local_sem,
):
    clus, n, y, rows, k = place()
    hb, ph = boxes // CORES, parents // CORES
    qb = hb // rows
    meet(clus, n, y, rows, k, True)
    partner = at_pair(clus, y, 1 - k)
    reach = range(1, REACH + 1)
    backward = range(REACH, -1, -1)
    keep, give = pl.ds(k * hb, hb), pl.ds((1 - k) * hb, hb)
    pkeep, pgive = pl.ds(k * ph, ph), pl.ds((1 - k) * ph, ph)
    local = pltpu.make_async_copy(basis_p, win.at[0], local_sem.at[0])
    plocal = pltpu.make_async_copy(pbasis_p, pwin.at[0], local_sem.at[1])
    local.start()
    plocal.start()

    core = [remote(far.at[o, give], half_in.at[o], (core_s, core_r), o, partner)
            for o in range(REACH + 1)]
    pcore = [remote(pfar.at[o, pgive], phalf_in.at[o], (pcore_s, pcore_r), o, partner)
             for o in range(REACH + 1)]
    down, pdown = {}, {}
    for o in reach:
        to = at_pair(clus - o, y, k)
        down[o] = remote(basis_p.at[keep], win.at[o, keep], (down_s, down_r), o, to)
        pdown[o] = remote(pbasis_p.at[pkeep], pwin.at[o, pkeep], (pdown_s, pdown_r), o, to)
    for o in backward:
        pcore[o].start()
        core[o].start()
    for o in reach:
        @pl.when(clus >= o)
        def _():
            pdown[o].start()
    for o in reach:
        @pl.when(clus >= o)
        def _():
            down[o].start()

    row = {}
    pup, up = {}, {}
    for o in backward:
        pcore[o].wait_recv()
        phalf[o] = pfar[o, pkeep] + phalf_in[o]
        if o:
            pup[o] = remote(phalf.at[o], pup_in.at[o - 1], (pup_s, pup_r), o, at_pair(clus + o, y, k))

            @pl.when(clus + o < n)
            def _():
                pup[o].start()
    for o in backward:
        core[o].wait_recv()
        half[o] = far[o, keep] + half_in[o]
        for d in range(1, rows):
            to = (y + d) % rows
            row[o, d] = remote(
                half.at[o, pl.ds(to * qb, qb)], row_in.at[o, d - 1], (row_s, row_r),
                o * (rows - 1) + d - 1, at_pair(clus, to, k),
            )
            row[o, d].start()
    for o in backward:
        total = half[o, pl.ds(y * qb, qb)]
        for d in range(1, rows):
            row[o, d].wait_recv()
            total = total + row_in[o, d - 1]
        mine[o] = total
        if o:
            up[o] = remote(mine.at[o], up_in.at[o - 1], (up_s, up_r), o, at_pair(clus + o, y, k))

            @pl.when(clus + o < n)
            def _():
                up[o].start()

    fwd, pfwd = {}, {}
    for o in reach:
        fwd[o] = remote(win.at[o, keep], win.at[o, keep], (fwd_s, fwd_r), o, partner)
        pfwd[o] = remote(pwin.at[o, pkeep], pwin.at[o, pkeep], (pfwd_s, pfwd_r), o, partner)
    for o in reach:
        @pl.when(clus + o < n)
        def _():
            pdown[o].wait_recv()
            pfwd[o].start()
    for o in reach:
        @pl.when(clus + o < n)
        def _():
            down[o].wait_recv()
            fwd[o].start()

    own[...] = mine[0]
    pown[...] = phalf[0]
    for o in reach:
        @pl.when(clus >= o)
        def _():
            pup[o].wait_recv()
            pown[...] += pup_in[o - 1]
            up[o].wait_recv()
            own[...] += up_in[o - 1]
    local.wait()
    plocal.wait()
    for o in reach:
        @pl.when(clus + o < n)
        def _():
            pfwd[o].wait()
            fwd[o].wait()
            up[o].wait_send()
            pup[o].wait_send()

        @pl.when(clus >= o)
        def _():
            down[o].wait_send()
            pdown[o].wait_send()
    for o in range(REACH + 1):
        core[o].wait_send()
        pcore[o].wait_send()
        for d in range(1, rows):
            row[o, d].wait_send()


def finish_kernel(
    boxes, parents,
    near, pnear, own, pown, transfer, child_parent,
    out,
    half_in, phalf_in, weight, pwork, total, row_in,
    core_s, core_r, pcore_s, pcore_r, pw_s, pw_r, row_s, row_r, gat_s, gat_r, fwd_s, fwd_r,
):
    clus, n, y, rows, k = place()
    hb, ph = boxes // CORES, parents // CORES
    qb = hb // rows
    meet(clus, n, y, rows, k, False)
    partner = at_pair(clus, y, 1 - k)
    pkeep, pgive = pl.ds(k * ph, ph), pl.ds((1 - k) * ph, ph)
    pcore = remote(pnear.at[pgive], phalf_in, (pcore_s, pcore_r), 0, partner)
    core = remote(near.at[pl.ds((1 - k) * hb, hb)], half_in, (core_s, core_r), 0, partner)
    pcore.start()
    core.start()
    pcore.wait_recv()
    pwork[...] = pnear[pkeep] + phalf_in[...] + pown[...]
    weight[pkeep] = pwork[...]
    pw = remote(pwork, weight.at[pkeep], (pw_s, pw_r), 0, partner)
    pw.start()
    core.wait_recv()
    total[...] = near[pl.ds(k * hb, hb)] + half_in[...]
    pw.wait_recv()

    def lower(b):
        c = k * hb + b
        w = unpack(weight[child_parent[0, c]])
        total[b] += pack(outer_product(transfer[c], w))

    row = []
    for d in list(range(1, rows)) + [0]:
        to = (y + d) % rows
        loop(qb, lambda q: lower(to * qb + q))
        if d:
            copy = remote(
                total.at[pl.ds(to * qb, qb)], row_in.at[d - 1], (row_s, row_r), d - 1,
                at_pair(clus, to, k),
            )
            copy.start()
            row.append(copy)
    result = total[pl.ds(y * qb, qb)] + own[...]
    for d in range(1, rows):
        row[d - 1].wait_recv()
        result = result + row_in[d - 1]
    here = pl.ds(k * hb + y * qb, qb)
    out[here] = result
    gather = [
        remote(out.at[here], out.at[here], (gat_s, gat_r), d - 1, at_pair(clus, (y + d) % rows, k))
        for d in range(1, rows)
    ]
    for copy in gather:
        copy.start()
    forward = []
    for d in range(rows):
        there = here
        if d:
            gather[d - 1].wait_recv()
            there = pl.ds(k * hb + (y + rows - d) % rows * qb, qb)
        copy = remote(out.at[there], out.at[there], (fwd_s, fwd_r), d, partner)
        copy.start()
        forward.append(copy)
    for copy in forward:
        copy.wait()
    for copy in gather + row + [core, pcore, pw]:
        copy.wait_send()


def unpack_kernel(packed, out):
    out[0] = unpack(packed[0])


def per_device(
    child_basis, transfer, child_parent, upper_weight, child_pairs, child_blocks,
    parent_pairs, parent_blocks,
):
    boxes, extent = child_basis.shape[0], child_basis.shape[-1]
    parents = upper_weight.shape[0]
    rows = lax.axis_size("pair") // CORES
    hb, ph = boxes // CORES, parents // CORES
    qb = hb // rows
    spans = REACH + 1
    tall = extent * 3 // 4
    shape = lambda *lead: jax.ShapeDtypeStruct(lead + (tall, extent), F32)
    room = lambda *lead: pltpu.VMEM(lead + (tall, extent), F32)
    sems = lambda *counts: [pltpu.SemaphoreType.DMA((c,)) for c in counts for _ in range(2)]

    pbasis, basis_p, pbasis_p, far, pfar = pl.pallas_call(
        functools.partial(far_kernel, boxes, parents),
        out_shape=(
            jax.ShapeDtypeStruct(upper_weight.shape, F32),
            shape(boxes), shape(parents), shape(spans * boxes), shape(spans * parents),
        ),
        in_specs=[VMEM, VMEM, SMEM, SMEM, VMEM, SMEM, VMEM],
        out_specs=(VMEM,) * 5,
        name="far_terms",
    )(child_basis, transfer, child_parent, child_pairs, child_blocks, parent_pairs, parent_blocks)

    win, pwin, own, pown = pl.pallas_call(
        functools.partial(exchange_kernel, boxes, parents),
        out_shape=(shape(spans, boxes), shape(spans, parents), shape(qb), shape(ph)),
        in_specs=[VMEM] * 4,
        out_specs=(VMEM,) * 4,
        scratch_shapes=[
            room(spans, hb), room(spans, ph), room(spans, hb), room(spans, ph),
            room(spans, max(rows - 1, 1), qb), room(spans, qb), room(REACH, qb), room(REACH, ph),
        ]
        + sems(spans, spans, spans, spans, spans * max(rows - 1, 1), spans, spans, spans, spans)
        + [pltpu.SemaphoreType.DMA((2,))],
        compiler_params=pltpu.CompilerParams(collective_id=0, has_side_effects=True),
        name="exchange",
    )(
        basis_p, pbasis_p,
        far.reshape(spans, boxes, tall, extent), pfar.reshape(spans, parents, tall, extent),
    )

    near, pnear = pl.pallas_call(
        functools.partial(near_kernel, boxes, parents, 1.0 / (rows * CORES)),
        out_shape=(shape(boxes), shape(parents)),
        in_specs=[SMEM, VMEM, VMEM, SMEM, VMEM, VMEM, VMEM],
        out_specs=(VMEM,) * 2,
        name="near_terms",
    )(
        child_pairs, child_blocks, win.reshape(spans * boxes, tall, extent),
        parent_pairs, parent_blocks, pwin.reshape(spans * parents, tall, extent), upper_weight,
    )

    packed = pl.pallas_call(
        functools.partial(finish_kernel, boxes, parents),
        out_shape=shape(boxes),
        in_specs=[VMEM] * 5 + [SMEM],
        out_specs=VMEM,
        scratch_shapes=[
            room(hb), room(ph), room(parents), room(ph), room(hb), room(max(rows - 1, 1), qb),
        ]
        + sems(1, 1, 1, max(rows - 1, 1), max(rows - 1, 1), rows),
        compiler_params=pltpu.CompilerParams(collective_id=1, has_side_effects=True),
        name="finish",
    )(near, pnear, own, pown, transfer, child_parent)

    child_weight = pl.pallas_call(
        unpack_kernel,
        grid=(boxes,),
        out_shape=jax.ShapeDtypeStruct(child_basis.shape, F32),
        in_specs=[pl.BlockSpec((1, tall, extent), lambda b: (b, 0, 0))],
        out_specs=pl.BlockSpec((1, extent, extent), lambda b: (b, 0, 0)),
        name="unfold",
    )(packed)
    return (child_weight, pbasis)


def solution(mesh):
    return jax.shard_map(
        per_device,
        mesh=mesh,
        in_specs=(
            P("clus", None, None),
            P("clus", None, None),
            P("clus", None),
            P("clus", None, None),
            P(("clus", "pair"), None),
            P(("clus", "pair"), None, None),
            P(("clus", "pair"), None),
            P(("clus", "pair"), None, None),
        ),
        out_specs=(P("clus", None, None), P("clus", None, None)),
        check_vma=False,
    )
```

time: 411 us -> 189 us (0.46)
  the two profiles are of different devices: /device:TPU:0 before, /device:TPU:3 now
where the time goes in v1:
time: 189 us
  Pallas kernels  185 us (98%)
  local copies, waits for them, and re-layouts  2.7 us (1%)
    pallas_call x1, Pallas kernels, per_device(): pl.pallas_call(functools.partial(exchange_kernel, boxes, parents), out_sh...  106 us
    pallas_call x1, Pallas kernels, per_device(): pl.pallas_call(functools.partial(finish_kernel, boxes, parents), out_shap...  29.8 us
    pallas_call x1, Pallas kernels, per_device(): pl.pallas_call(functools.partial(far_kernel, boxes, parents), out_shape=(...  25.4 us
    pallas_call x1, Pallas kernels, per_device(): pl.pallas_call(functools.partial(near_kernel, boxes, parents, 1.0 / (rows...  17.8 us
    pallas_call x1, Pallas kernels, per_device(): pl.pallas_call(unpack_kernel, grid=(boxes,), out_shape=jax.ShapeDtypeStru...  5.86 us

profile of v1, /device:TPU:3, one launch (start us, length us, event | category | flops | bytes accessed | tf_op | source)
XLA Modules:
  0.0 188.7 jit_solution(16515343390723557404)
XLA Ops:
  0.6 1.3 copy.11.ppairs
  2.0 1.4 copy.12.cpairs
  3.3 25.4 %far_terms.1 = (f32[2,256,256]{2,1,0:T(8,128)}, f32[8,192,256]{2,1,0:T(8,128)}, f32[2,192,256]{2,1,0:T(8,128)}, f32[32,192,256]{2,1,0:T(8,128)}, f32[8,192,256]{2,1,0:T(8,128)}) custom-call(f32[8,256,256]{2,1,0:T(8,128)} %basis.1, f32[8,256,256]{2,1,0:T(8,128)} %transfer.3, s32[1,8]{1,0:T(1,128)} %child_parent.3, s32[12,2]{1,0:T(8,128)} %copy.12.cpairs, ...), custom_call_target="tpu_custom_call" | custom-call | tf_op jit(solution)/shard_map/far_terms/pallas_call | solution.py:374
  28.8 106.5 %exchange.1 = (f32[4,8,192,256]{3,2,1,0:T(8,128)}, f32[4,2,192,256]{3,2,1,0:T(8,128)}, f32[2,192,256]{2,1,0:T(8,128)}, f32[1,192,256]{2,1,0:T(8,128)}) custom-call(f32[8,192,256]{2,1,0:T(8,128)} %get-tuple-element.13.basis_p, f32[2,192,256]{2,1,0:T(8,128)} %get-tuple-element.14.pbasis_p, f32[4,8,192,256]{3,2,1,0:T(8,128)} %bitcast.5, f32[4,2,192,256]{3,2,1,0:T(8,128)} %bitcast.6), custom_call_target="tpu_custom_call" | custom-call | tf_op jit(solution)/shard_map/exchange/pallas_call | solution.py:385
  135.2 17.8 %near_terms.1 = (f32[8,192,256]{2,1,0:T(8,128)}, f32[2,192,256]{2,1,0:T(8,128)}) custom-call(s32[12,2]{1,0:T(8,128)} %copy.12.cpairs, f32[12,256,256]{2,1,0:T(8,128)} %cblocks.3, f32[32,192,256]{2,1,0:T(8,128)} %bitcast.4, s32[8,2]{1,0:T(8,128)} %copy.11.ppairs, f32[8,256,256]{2,1,0:T(8,128)} %pblocks.3, f32[8,192,256]{2,1,0:T(8,128)} %bitcast.7, ...), custom_call_target="tpu_custom_call" | custom-call | tf_op jit(solution)/shard_map/near_terms/pallas_call | solution.py:403
  153.0 29.8 %finish.1.packed = f32[8,192,256]{2,1,0:T(8,128)} custom-call(f32[8,192,256]{2,1,0:T(8,128)} %get-tuple-element.19.near, f32[2,192,256]{2,1,0:T(8,128)} %get-tuple-element.20.pnear, f32[2,192,256]{2,1,0:T(8,128)} %get-tuple-element.21.own, f32[1,192,256]{2,1,0:T(8,128)} %get-tuple-element.22.pown, f32[8,256,256]{2,1,0:T(8,128)} %transfer.3, s32[1,8]{1,0:T(1,128)} %child_parent.3), custom_call_target="tpu_custom_call" | custom-call | tf_op jit(solution)/shard_map/finish/pallas_call | solution.py:414
  182.9 5.9 %unfold.1 = f32[8,256,256]{2,1,0:T(8,128)} custom-call(f32[8,192,256]{2,1,0:T(8,128)} %finish.1.packed), custom_call_target="tpu_custom_call" | custom-call | tf_op jit(solution)/shard_map/unfold/pallas_call | solution.py:427

commit v2 on v1

--- a/solution.py
+++ b/solution.py
@@ -166,8 +166,8 @@
     basis_p, pbasis_p, far, pfar,
     win, pwin, own, pown,
     half_in, phalf_in, half, phalf, row_in, mine, up_in, pup_in,
-    down_s, down_r, pdown_s, pdown_r, core_s, core_r, pcore_s, pcore_r,
-    row_s, row_r, up_s, up_r, pup_s, pup_r, fwd_s, fwd_r, pfwd_s, pfwd_r, local_sem,
+    down_s, down_r, fwd_s, fwd_r, core_s, core_r, pcore_s, pcore_r,
+    row_s, row_r, up_s, up_r, pup_s, pup_r, local_sem,
 ):
     clus, n, y, rows, k = place()
     hb, ph = boxes // CORES, parents // CORES
@@ -175,7 +175,9 @@
     meet(clus, n, y, rows, k, True)
     partner = at_pair(clus, y, 1 - k)
     reach = range(1, REACH + 1)
-    backward = range(REACH, -1, -1)
+    order = (3, 1, 2, 0)
+    odd = clus % 2 == 1
+    even = clus % 2 == 0
     keep, give = pl.ds(k * hb, hb), pl.ds((1 - k) * hb, hb)
     pkeep, pgive = pl.ds(k * ph, ph), pl.ds((1 - k) * ph, ph)
     local = pltpu.make_async_copy(basis_p, win.at[0], local_sem.at[0])
@@ -183,39 +185,72 @@
     local.start()
     plocal.start()
 
+    chunks = range(hb + 1)
+
+    def held(o, i):
+        return pwin.at[o, pkeep] if i == 0 else win.at[o, pl.ds(k * hb + i - 1, 1)]
+
+    def first(i):
+        return pbasis_p.at[pkeep] if i == 0 else basis_p.at[pl.ds(k * hb + i - 1, 1)]
+
+    def down(src, o, i, to):
+        return remote(src, held(o, i), (down_s, down_r), o * (hb + 1) + i, at_pair(to, y, k))
+
+    def to_two(i):
+        return down(first(i), 2, i, clus - 2)
+
+    def to_one(i):
+        return down(first(i), 1, i, clus - 1)
+
+    def side(i):
+        return down(held(2, i), 1, i, clus + 1)
+
+    def to_three(i):
+        return down(held(1, i), 3, i, clus - 2)
+
+    def forward(o, i):
+        return remote(held(o, i), held(o, i), (fwd_s, fwd_r), o * (hb + 1) + i, partner)
+
     core = [remote(far.at[o, give], half_in.at[o], (core_s, core_r), o, partner)
             for o in range(REACH + 1)]
     pcore = [remote(pfar.at[o, pgive], phalf_in.at[o], (pcore_s, pcore_r), o, partner)
              for o in range(REACH + 1)]
-    down, pdown = {}, {}
-    for o in reach:
-        to = at_pair(clus - o, y, k)
-        down[o] = remote(basis_p.at[keep], win.at[o, keep], (down_s, down_r), o, to)
-        pdown[o] = remote(pbasis_p.at[pkeep], pwin.at[o, pkeep], (pdown_s, pdown_r), o, to)
-    for o in backward:
+    for i in chunks:
+        @pl.when(clus >= 2)
+        def _():
+            to_two(i).start()
+
+        @pl.when(odd)
+        def _():
+            to_one(i).start()
+    for o in order:
+        core[o].start()
+    for o in order:
         pcore[o].start()
-        core[o].start()
-    for o in reach:
-        @pl.when(clus >= o)
-        def _():
-            pdown[o].start()
-    for o in reach:
-        @pl.when(clus >= o)
-        def _():
-            down[o].start()
+
+    def pass_on(i):
+        @pl.when(clus + 2 < n)
+        def _():
+            to_two(i).wait_recv()
+
+            @pl.when(even)
+            def _():
+                side(i).start()
+
+            forward(2, i).start()
+
+        @pl.when(clus + 1 < n)
+        def _():
+            to_one(i).wait_recv()
+
+            @pl.when(clus >= 2)
+            def _():
+                to_three(i).start()
+
+            forward(1, i).start()
 
     row = {}
-    pup, up = {}, {}
-    for o in backward:
-        pcore[o].wait_recv()
-        phalf[o] = pfar[o, pkeep] + phalf_in[o]
-        if o:
-            pup[o] = remote(phalf.at[o], pup_in.at[o - 1], (pup_s, pup_r), o, at_pair(clus + o, y, k))
-
-            @pl.when(clus + o < n)
-            def _():
-                pup[o].start()
-    for o in backward:
+    for o in order:
         core[o].wait_recv()
         half[o] = far[o, keep] + half_in[o]
         for d in range(1, rows):
@@ -225,33 +260,69 @@
                 o * (rows - 1) + d - 1, at_pair(clus, to, k),
             )
             row[o, d].start()
-    for o in backward:
+    pup = {}
+    for o in order:
+        pcore[o].wait_recv()
+        phalf[o] = pfar[o, pkeep] + phalf_in[o]
+        if o:
+            pup[o] = remote(phalf.at[o], pup_in.at[o - 1], (pup_s, pup_r), o, at_pair(clus + o, y, k))
+
+            @pl.when(clus + o < n)
+            def _():
+                pup[o].start()
+
+    def up(o, slot, to):
+        return remote(mine.at[o], up_in.at[slot], (up_s, up_r), slot, at_pair(to, y, k))
+
+    def gathered(o):
         total = half[o, pl.ds(y * qb, qb)]
         for d in range(1, rows):
             row[o, d].wait_recv()
             total = total + row_in[o, d - 1]
         mine[o] = total
-        if o:
-            up[o] = remote(mine.at[o], up_in.at[o - 1], (up_s, up_r), o, at_pair(clus + o, y, k))
-
-            @pl.when(clus + o < n)
-            def _():
-                up[o].start()
-
-    fwd, pfwd = {}, {}
-    for o in reach:
-        fwd[o] = remote(win.at[o, keep], win.at[o, keep], (fwd_s, fwd_r), o, partner)
-        pfwd[o] = remote(pwin.at[o, pkeep], pwin.at[o, pkeep], (pfwd_s, pfwd_r), o, partner)
-    for o in reach:
-        @pl.when(clus + o < n)
-        def _():
-            pdown[o].wait_recv()
-            pfwd[o].start()
-    for o in reach:
-        @pl.when(clus + o < n)
-        def _():
-            down[o].wait_recv()
-            fwd[o].start()
+
+    def rise(o):
+        gathered(o)
+        if o == 3:
+            @pl.when(clus + 3 < n)
+            def _():
+                up(3, 3, clus + 2).start()
+        if o == 1:
+            @pl.when((clus >= 2) & (clus + 1 < n))
+            def _():
+                up(3, 3, clus + 2).wait_recv()
+                mine[1] += up_in[3]
+
+            @pl.when(even & (clus + 1 < n))
+            def _():
+                up(1, 1, clus + 1).start()
+
+            @pl.when(odd & (clus + 1 < n))
+            def _():
+                up(1, 0, clus - 1).start()
+        if o == 2:
+            @pl.when(even & (clus + 2 < n))
+            def _():
+                up(1, 0, clus - 1).wait_recv()
+                mine[2] += up_in[0]
+
+            @pl.when(clus + 2 < n)
+            def _():
+                up(2, 2, clus + 2).start()
+
+    pass_on(0)
+    todo = list(order)
+    for i in chunks[1:]:
+        pass_on(i)
+        if todo:
+            rise(todo.pop(0))
+    for o in todo:
+        rise(o)
+    for i in chunks:
+        @pl.when(clus + 3 < n)
+        def _():
+            to_three(i).wait_recv()
+            forward(3, i).start()
 
     own[...] = mine[0]
     pown[...] = phalf[0]
@@ -260,22 +331,61 @@
         def _():
             pup[o].wait_recv()
             pown[...] += pup_in[o - 1]
-            up[o].wait_recv()
-            own[...] += up_in[o - 1]
+
+    @pl.when(odd)
+    def _():
+        up(1, 1, clus + 1).wait_recv()
+        own[...] += up_in[1]
+
+    @pl.when(clus >= 2)
+    def _():
+        up(2, 2, clus + 2).wait_recv()
+        own[...] += up_in[2]
+
     local.wait()
     plocal.wait()
+    for i in chunks:
+        @pl.when(clus >= 2)
+        def _():
+            to_two(i).wait_send()
+
+            @pl.when(clus + 1 < n)
+            def _():
+                to_three(i).wait_send()
+
+        @pl.when(odd)
+        def _():
+            to_one(i).wait_send()
+
+        @pl.when(even & (clus + 2 < n))
+        def _():
+            side(i).wait_send()
+
+        for o in reach:
+            @pl.when(clus + o < n)
+            def _():
+                forward(o, i).wait()
     for o in reach:
         @pl.when(clus + o < n)
         def _():
-            pfwd[o].wait()
-            fwd[o].wait()
-            up[o].wait_send()
             pup[o].wait_send()
 
-        @pl.when(clus >= o)
-        def _():
-            down[o].wait_send()
-            pdown[o].wait_send()
+    @pl.when(clus + 3 < n)
+    def _():
+        up(3, 3, clus + 2).wait_send()
+
+    @pl.when(clus + 2 < n)
+    def _():
+        up(2, 2, clus + 2).wait_send()
+
+    @pl.when(even & (clus + 1 < n))
+    def _():
+        up(1, 1, clus + 1).wait_send()
+
+    @pl.when(odd & (clus + 1 < n))
+    def _():
+        up(1, 0, clus - 1).wait_send()
+
     for o in range(REACH + 1):
         core[o].wait_send()
         pcore[o].wait_send()
@@ -389,9 +499,11 @@
         out_specs=(VMEM,) * 4,
         scratch_shapes=[
             room(spans, hb), room(spans, ph), room(spans, hb), room(spans, ph),
-            room(spans, max(rows - 1, 1), qb), room(spans, qb), room(REACH, qb), room(REACH, ph),
+            room(spans, max(rows - 1, 1), qb), room(spans, qb), room(spans, qb), room(REACH, ph),
         ]
-        + sems(spans, spans, spans, spans, spans * max(rows - 1, 1), spans, spans, spans, spans)
+        + sems(
+            spans * (hb + 1), spans * (hb + 1), spans, spans, spans * max(rows - 1, 1), spans, spans
+        )
         + [pltpu.SemaphoreType.DMA((2,))],
         compiler_params=pltpu.CompilerParams(collective_id=0, has_side_effects=True),
         name="exchange",

time: 189 us -> 149 us (0.79)
  the two profiles are of different devices: /device:TPU:3 before, /device:TPU:19 now
where the time goes in v2:
time: 149 us; the launch traced here: 146 us
  Pallas kernels  143 us (96%)
  local copies, waits for them, and re-layouts  2.7 us (2%)
    pallas_call x1, Pallas kernels, per_device(): pl.pallas_call(functools.partial(exchange_kernel, boxes, parents), out_sh...  60.6 us
    pallas_call x1, Pallas kernels, per_device(): pl.pallas_call(functools.partial(finish_kernel, boxes, parents), out_shap...  33 us
    pallas_call x1, Pallas kernels, per_device(): pl.pallas_call(functools.partial(far_kernel, boxes, parents), out_shape=(...  25.4 us
    pallas_call x1, Pallas kernels, per_device(): pl.pallas_call(functools.partial(near_kernel, boxes, parents, 1.0 / (rows...  17.8 us
    pallas_call x1, Pallas kernels, per_device(): pl.pallas_call(unpack_kernel, grid=(boxes,), out_shape=jax.ShapeDtypeStru...  5.86 us

profile of v2, /device:TPU:19, one launch (start us, length us, event | category | flops | bytes accessed | tf_op | source)
XLA Modules:
  0.0 146.0 jit_solution(5412483208143239646)
XLA Ops:
  0.6 1.3 copy.11.ppairs
  2.0 1.4 copy.12.cpairs
  3.3 25.4 %far_terms.1 = (f32[2,256,256]{2,1,0:T(8,128)}, f32[8,192,256]{2,1,0:T(8,128)}, f32[2,192,256]{2,1,0:T(8,128)}, f32[32,192,256]{2,1,0:T(8,128)}, f32[8,192,256]{2,1,0:T(8,128)}) custom-call(f32[8,256,256]{2,1,0:T(8,128)} %basis.1, f32[8,256,256]{2,1,0:T(8,128)} %transfer.3, s32[1,8]{1,0:T(1,128)} %child_parent.3, s32[12,2]{1,0:T(8,128)} %copy.12.cpairs, ...), custom_call_target="tpu_custom_call" | custom-call | tf_op jit(solution)/shard_map/far_terms/pallas_call | solution.py:484
  28.8 60.6 %exchange.1 = (f32[4,8,192,256]{3,2,1,0:T(8,128)}, f32[4,2,192,256]{3,2,1,0:T(8,128)}, f32[2,192,256]{2,1,0:T(8,128)}, f32[1,192,256]{2,1,0:T(8,128)}) custom-call(f32[8,192,256]{2,1,0:T(8,128)} %get-tuple-element.13.basis_p, f32[2,192,256]{2,1,0:T(8,128)} %get-tuple-element.14.pbasis_p, f32[4,8,192,256]{3,2,1,0:T(8,128)} %bitcast.5, f32[4,2,192,256]{3,2,1,0:T(8,128)} %bitcast.6), custom_call_target="tpu_custom_call" | custom-call | tf_op jit(solution)/shard_map/exchange/pallas_call | solution.py:495
  89.4 17.8 %near_terms.1 = (f32[8,192,256]{2,1,0:T(8,128)}, f32[2,192,256]{2,1,0:T(8,128)}) custom-call(s32[12,2]{1,0:T(8,128)} %copy.12.cpairs, f32[12,256,256]{2,1,0:T(8,128)} %cblocks.3, f32[32,192,256]{2,1,0:T(8,128)} %bitcast.4, s32[8,2]{1,0:T(8,128)} %copy.11.ppairs, f32[8,256,256]{2,1,0:T(8,128)} %pblocks.3, f32[8,192,256]{2,1,0:T(8,128)} %bitcast.7, ...), custom_call_target="tpu_custom_call" | custom-call | tf_op jit(solution)/shard_map/near_terms/pallas_call | solution.py:515
  107.2 33.0 %finish.1.packed = f32[8,192,256]{2,1,0:T(8,128)} custom-call(f32[8,192,256]{2,1,0:T(8,128)} %get-tuple-element.19.near, f32[2,192,256]{2,1,0:T(8,128)} %get-tuple-element.20.pnear, f32[2,192,256]{2,1,0:T(8,128)} %get-tuple-element.21.own, f32[1,192,256]{2,1,0:T(8,128)} %get-tuple-element.22.pown, f32[8,256,256]{2,1,0:T(8,128)} %transfer.3, s32[1,8]{1,0:T(1,128)} %child_parent.3), custom_call_target="tpu_custom_call" | custom-call | tf_op jit(solution)/shard_map/finish/pallas_call | solution.py:526
  140.2 5.9 %unfold.1 = f32[8,256,256]{2,1,0:T(8,128)} custom-call(f32[8,192,256]{2,1,0:T(8,128)} %finish.1.packed), custom_call_target="tpu_custom_call" | custom-call | tf_op jit(solution)/shard_map/unfold/pallas_call | solution.py:539

commit v3 on v2

--- a/solution.py
+++ b/solution.py
@@ -62,64 +62,30 @@
     return product(s, split(product(g, s, NN)), TN)
 
 
-def far_kernel(
-    boxes, parents,
-    basis, transfer, child_parent, cpairs, cblocks, ppairs, pblocks,
-    pbasis, basis_p, pbasis_p, far, pfar,
-):
-    clus = lax.axis_index("clus")
-    pbasis[...] = jnp.zeros_like(pbasis)
-    far[...] = jnp.zeros_like(far)
-    pfar[...] = jnp.zeros_like(pfar)
-
-    def lift(c):
-        g = basis[c]
-        basis_p[c] = pack(g)
-        p = child_parent[0, c]
-        pbasis[p] += inner_product(transfer[c], g)
-
-    loop(boxes, lift)
-
-    def terms(pairs, blocks, grams, sums, count):
-        def one(r):
-            i, j = pairs[r, 0], pairs[r, 1]
-
-            @pl.when(i >= 0)
-            def _():
-                t = inner_product(blocks[r], grams[i - clus * count])
-                sums[j - clus * count] += pack(t)
-
-        loop(blocks.shape[0], one)
-
-    for p in range(parents):
-        pbasis_p[p] = pack(pbasis[p])
-    terms(ppairs, pblocks, pbasis, pfar, parents)
-    terms(cpairs, cblocks, basis, far, boxes)
-
-
-def near_kernel(
-    boxes, parents, scale,
-    cpairs, cblocks, win, ppairs, pblocks, pwin, upper,
-    near, pnear,
-):
-    clus = lax.axis_index("clus")
-    near[...] = jnp.zeros_like(near)
-    for p in range(parents):
-        pnear[p] = pack(upper[p]) * scale
-
-    def terms(pairs, blocks, grams, sums, count):
-        def one(r):
-            i, j = pairs[r, 0], pairs[r, 1]
-
-            @pl.when(i >= 0)
-            def _():
-                t = outer_product(blocks[r], unpack(grams[j - clus * count]))
-                sums[i - clus * count] += pack(t)
-
-        loop(blocks.shape[0], one)
-
-    terms(ppairs, pblocks, pwin, pnear, parents)
-    terms(cpairs, cblocks, win, near, boxes)
+def spread(terms, slots, sums, count, weights):
+    tall = terms.shape[1]
+    step = tall // 6
+
+    def two(t):
+        picks = [
+            [((slots(r) == 2 * t + e) & weights(r)).astype(F32) for r in range(terms.shape[0])]
+            for e in range(2)
+        ]
+
+        def part(i):
+            at = pl.ds(pl.multiple_of(i * step, step), step)
+            totals = [None, None]
+            for r in range(terms.shape[0]):
+                value = terms[r, at, :]
+                for e in range(2):
+                    add = value * picks[e][r]
+                    totals[e] = add if totals[e] is None else totals[e] + add
+            for e in range(2):
+                sums[2 * t + e, at, :] = totals[e]
+
+        loop(6, part)
+
+    loop(count // 2, two)
 
 
 def remote(src, dst, sems, index, device):
@@ -162,36 +128,35 @@
 
 
 def exchange_kernel(
-    boxes, parents,
-    basis_p, pbasis_p, far, pfar,
-    win, pwin, own, pown,
+    boxes, parents, scale,
+    basis, transfer, child_parent, cpairs, cblocks, ppairs, pblocks, upper,
+    pbasis, near, pnear, own, pown,
+    win, pwin, terms, pterms, far, pfar,
     half_in, phalf_in, half, phalf, row_in, mine, up_in, pup_in,
     down_s, down_r, fwd_s, fwd_r, core_s, core_r, pcore_s, pcore_r,
-    row_s, row_r, up_s, up_r, pup_s, pup_r, local_sem,
+    row_s, row_r, up_s, up_r, pup_s, pup_r,
 ):
     clus, n, y, rows, k = place()
     hb, ph = boxes // CORES, parents // CORES
     qb = hb // rows
+    loop(boxes, lambda c: win.__setitem__(c, pack(basis[c])))
     meet(clus, n, y, rows, k, True)
     partner = at_pair(clus, y, 1 - k)
     reach = range(1, REACH + 1)
     order = (3, 1, 2, 0)
     odd = clus % 2 == 1
     even = clus % 2 == 0
-    keep, give = pl.ds(k * hb, hb), pl.ds((1 - k) * hb, hb)
-    pkeep, pgive = pl.ds(k * ph, ph), pl.ds((1 - k) * ph, ph)
-    local = pltpu.make_async_copy(basis_p, win.at[0], local_sem.at[0])
-    plocal = pltpu.make_async_copy(pbasis_p, pwin.at[0], local_sem.at[1])
-    local.start()
-    plocal.start()
+    pkeep = pl.ds(k * ph, ph)
 
     chunks = range(hb + 1)
 
     def held(o, i):
-        return pwin.at[o, pkeep] if i == 0 else win.at[o, pl.ds(k * hb + i - 1, 1)]
+        if i == hb:
+            return pwin.at[pl.ds(o * parents + k * ph, ph)]
+        return win.at[pl.ds(o * boxes + k * hb + i, 1)]
 
     def first(i):
-        return pbasis_p.at[pkeep] if i == 0 else basis_p.at[pl.ds(k * hb + i - 1, 1)]
+        return held(0, i)
 
     def down(src, o, i, to):
         return remote(src, held(o, i), (down_s, down_r), o * (hb + 1) + i, at_pair(to, y, k))
@@ -211,11 +176,12 @@
     def forward(o, i):
         return remote(held(o, i), held(o, i), (fwd_s, fwd_r), o * (hb + 1) + i, partner)
 
-    core = [remote(far.at[o, give], half_in.at[o], (core_s, core_r), o, partner)
+    core = [remote(far.at[pl.ds(o * boxes + (1 - k) * hb, hb)], half_in.at[o], (core_s, core_r), o, partner)
             for o in range(REACH + 1)]
-    pcore = [remote(pfar.at[o, pgive], phalf_in.at[o], (pcore_s, pcore_r), o, partner)
+    pcore = [remote(pfar.at[pl.ds(o * parents + (1 - k) * ph, ph)], phalf_in.at[o], (pcore_s, pcore_r), o, partner)
              for o in range(REACH + 1)]
-    for i in chunks:
+
+    def launch(i):
         @pl.when(clus >= 2)
         def _():
             to_two(i).start()
@@ -223,36 +189,80 @@
         @pl.when(odd)
         def _():
             to_one(i).start()
+
+    def pass_on(i):
+        @pl.when(clus + 2 < n)
+        def _():
+            to_two(i).wait_recv()
+
+            @pl.when(even)
+            def _():
+                side(i).start()
+
+            forward(2, i).start()
+
+        @pl.when(clus + 1 < n)
+        def _():
+            to_one(i).wait_recv()
+
+            @pl.when(clus >= 2)
+            def _():
+                to_three(i).start()
+
+            forward(1, i).start()
+
+    def usable(pairs):
+        return lambda r: pairs[r, 0] >= 0
+
+    def slot(pairs, side, count):
+        return lambda r: pairs[r, side] - clus * count
+
+    def inner(pairs, blocks, grams, count, out, start, stop):
+        def one(t):
+            r = start + t
+            i = jnp.clip(pairs[r, 0] - clus * count, 0, count - 1)
+            out[r] = pack(inner_product(blocks[r], grams[i]))
+
+        loop(stop - start, one)
+
+    def outer(pairs, blocks, grams, count, out):
+        def one(r):
+            j = jnp.clip(pairs[r, 1] - clus * count, 0, grams.shape[0] - 1)
+            j = jnp.where(pairs[r, 0] >= 0, j, 0)
+            out[r] = pack(outer_product(blocks[r], unpack(grams[j])))
+
+        loop(blocks.shape[0], one)
+
+    slots = cblocks.shape[0]
+    for i in range(hb):
+        launch(i)
+    pbasis[...] = jnp.zeros_like(pbasis)
+
+    def lift(c):
+        t = inner_product(transfer[c], basis[c])
+        for p in range(parents):
+            pbasis[p] += t * (child_parent[0, c] == p).astype(F32)
+
+    loop(boxes, lift)
+    for p in range(parents):
+        pwin[p] = pack(pbasis[p])
+    launch(hb)
+    inner(cpairs, cblocks, basis, boxes, terms, 0, slots // 2)
+    pass_on(0)
+    pass_on(1)
+    inner(cpairs, cblocks, basis, boxes, terms, slots // 2, slots)
+    spread(terms, slot(cpairs, 1, boxes), far, (REACH + 1) * boxes, usable(cpairs))
     for o in order:
         core[o].start()
+    pass_on(2)
+    inner(ppairs, pblocks, pbasis, parents, pterms, 0, pblocks.shape[0])
+    spread(pterms, slot(ppairs, 1, parents), pfar, (REACH + 1) * parents, usable(ppairs))
     for o in order:
         pcore[o].start()
-
-    def pass_on(i):
-        @pl.when(clus + 2 < n)
-        def _():
-            to_two(i).wait_recv()
-
-            @pl.when(even)
-            def _():
-                side(i).start()
-
-            forward(2, i).start()
-
-        @pl.when(clus + 1 < n)
-        def _():
-            to_one(i).wait_recv()
-
-            @pl.when(clus >= 2)
-            def _():
-                to_three(i).start()
-
-            forward(1, i).start()
-
     row = {}
     for o in order:
         core[o].wait_recv()
-        half[o] = far[o, keep] + half_in[o]
+        half[o] = far[pl.ds(o * boxes + k * hb, hb)] + half_in[o]
         for d in range(1, rows):
             to = (y + d) % rows
             row[o, d] = remote(
@@ -263,7 +273,7 @@
     pup = {}
     for o in order:
         pcore[o].wait_recv()
-        phalf[o] = pfar[o, pkeep] + phalf_in[o]
+        phalf[o] = pfar[pl.ds(o * parents + k * ph, ph)] + phalf_in[o]
         if o:
             pup[o] = remote(phalf.at[o], pup_in.at[o - 1], (pup_s, pup_r), o, at_pair(clus + o, y, k))
 
@@ -310,20 +320,34 @@
             def _():
                 up(2, 2, clus + 2).start()
 
-    pass_on(0)
-    todo = list(order)
-    for i in chunks[1:]:
+    pass_on(hb)
+    for i in range(3, hb):
         pass_on(i)
-        if todo:
-            rise(todo.pop(0))
-    for o in todo:
-        rise(o)
-    for i in chunks:
+    rise(3)
+
+    def settle(i):
         @pl.when(clus + 3 < n)
         def _():
             to_three(i).wait_recv()
             forward(3, i).start()
 
+    settle(hb)
+    rise(1)
+    for i in range(hb):
+        settle(i)
+    for i in chunks:
+        for o in reach:
+            @pl.when(clus + o < n)
+            def _():
+                forward(o, i).wait_recv()
+    outer(ppairs, pblocks, pwin, parents, pterms)
+    spread(pterms, slot(ppairs, 0, parents), pnear, parents, usable(ppairs))
+    for p in range(parents):
+        pnear[p] += pack(upper[p]) * scale
+    rise(2)
+    outer(cpairs, cblocks, win, boxes, terms)
+    spread(terms, slot(cpairs, 0, boxes), near, boxes, usable(cpairs))
+    rise(0)
     own[...] = mine[0]
     pown[...] = phalf[0]
     for o in reach:
@@ -342,8 +366,6 @@
         up(2, 2, clus + 2).wait_recv()
         own[...] += up_in[2]
 
-    local.wait()
-    plocal.wait()
     for i in chunks:
         @pl.when(clus >= 2)
         def _():
@@ -364,7 +386,7 @@
         for o in reach:
             @pl.when(clus + o < n)
             def _():
-                forward(o, i).wait()
+                forward(o, i).wait_send()
     for o in reach:
         @pl.when(clus + o < n)
         def _():
@@ -481,46 +503,29 @@
     room = lambda *lead: pltpu.VMEM(lead + (tall, extent), F32)
     sems = lambda *counts: [pltpu.SemaphoreType.DMA((c,)) for c in counts for _ in range(2)]
 
-    pbasis, basis_p, pbasis_p, far, pfar = pl.pallas_call(
-        functools.partial(far_kernel, boxes, parents),
+    cslots, pslots = child_blocks.shape[0], parent_blocks.shape[0]
+    pbasis, near, pnear, own, pown = pl.pallas_call(
+        functools.partial(exchange_kernel, boxes, parents, 1.0 / (rows * CORES)),
         out_shape=(
             jax.ShapeDtypeStruct(upper_weight.shape, F32),
-            shape(boxes), shape(parents), shape(spans * boxes), shape(spans * parents),
+            shape(boxes), shape(parents), shape(qb), shape(ph),
         ),
-        in_specs=[VMEM, VMEM, SMEM, SMEM, VMEM, SMEM, VMEM],
+        in_specs=[VMEM, VMEM, SMEM, SMEM, VMEM, SMEM, VMEM, VMEM],
         out_specs=(VMEM,) * 5,
-        name="far_terms",
-    )(child_basis, transfer, child_parent, child_pairs, child_blocks, parent_pairs, parent_blocks)
-
-    win, pwin, own, pown = pl.pallas_call(
-        functools.partial(exchange_kernel, boxes, parents),
-        out_shape=(shape(spans, boxes), shape(spans, parents), shape(qb), shape(ph)),
-        in_specs=[VMEM] * 4,
-        out_specs=(VMEM,) * 4,
         scratch_shapes=[
+            room(spans * boxes), room(spans * parents), room(cslots), room(pslots),
+            room(spans * boxes), room(spans * parents),
             room(spans, hb), room(spans, ph), room(spans, hb), room(spans, ph),
             room(spans, max(rows - 1, 1), qb), room(spans, qb), room(spans, qb), room(REACH, ph),
         ]
         + sems(
             spans * (hb + 1), spans * (hb + 1), spans, spans, spans * max(rows - 1, 1), spans, spans
-        )
-        + [pltpu.SemaphoreType.DMA((2,))],
+        ),
         compiler_params=pltpu.CompilerParams(collective_id=0, has_side_effects=True),
         name="exchange",
     )(
-        basis_p, pbasis_p,
-        far.reshape(spans, boxes, tall, extent), pfar.reshape(spans, parents, tall, extent),
-    )
-
-    near, pnear = pl.pallas_call(
-        functools.partial(near_kernel, boxes, parents, 1.0 / (rows * CORES)),
-        out_shape=(shape(boxes), shape(parents)),
-        in_specs=[SMEM, VMEM, VMEM, SMEM, VMEM, VMEM, VMEM],
-        out_specs=(VMEM,) * 2,
-        name="near_terms",
-    )(
-        child_pairs, child_blocks, win.reshape(spans * boxes, tall, extent),
-        parent_pairs, parent_blocks, pwin.reshape(spans * parents, tall, extent), upper_weight,
+        child_basis, transfer, child_parent, child_pairs, child_blocks, parent_pairs,
+        parent_blocks, upper_weight,
     )
 
     packed = pl.pallas_call(

time: 149 us -> 136 us (0.913)
  the two profiles are of different devices: /device:TPU:19 before, /device:TPU:17 now
where the time goes in v3:
time: 136 us
  Pallas kernels  132 us (97%)
  local copies, waits for them, and re-layouts  3.5 us (3%)
    pallas_call x1, Pallas kernels, per_device(): pl.pallas_call(functools.partial(exchange_kernel, boxes, parents, 1.0 / (...  93.9 us
    pallas_call x1, Pallas kernels, per_device(): pl.pallas_call(functools.partial(finish_kernel, boxes, parents), out_shap...  32.1 us
    pallas_call x1, Pallas kernels, per_device(): pl.pallas_call(unpack_kernel, grid=(boxes,), out_shape=jax.ShapeDtypeStru...  5.92 us
    unnamed x5, local copies, waits for them, and re-layouts  3.5 us

profile of v3, /device:TPU:17, one launch (start us, length us, event | category | flops | bytes accessed | tf_op | source)
XLA Modules:
  0.0 136.1 jit_solution(18396824500539687992)
XLA Ops:
  0.6 1.3 copy.11.ppairs
  2.0 1.4 copy.10.cpairs
  3.3 93.9 %exchange.1 = (f32[2,256,256]{2,1,0:T(8,128)}, f32[8,192,256]{2,1,0:T(8,128)}, f32[2,192,256]{2,1,0:T(8,128)}, f32[2,192,256]{2,1,0:T(8,128)}, f32[1,192,256]{2,1,0:T(8,128)}) custom-call(f32[8,256,256]{2,1,0:T(8,128)} %basis.1, f32[8,256,256]{2,1,0:T(8,128)} %transfer.3, s32[1,8]{1,0:T(1,128)} %child_parent.3, s32[12,2]{1,0:T(8,128)} %copy.10.cpairs, ...), custom_call_target="tpu_custom_call" | custom-call | tf_op jit(solution)/shard_map/exchange/pallas_call | solution.py:507
  97.2 32.1 %finish.1.packed = f32[8,192,256]{2,1,0:T(8,128)} custom-call(f32[8,192,256]{2,1,0:T(8,128)} %get-tuple-element.7.near, f32[2,192,256]{2,1,0:T(8,128)} %get-tuple-element.8.pnear, f32[2,192,256]{2,1,0:T(8,128)} %get-tuple-element.9.own, f32[1,192,256]{2,1,0:T(8,128)} %get-tuple-element.10.pown, f32[8,256,256]{2,1,0:T(8,128)} %transfer.3, s32[1,8]{1,0:T(1,128)} %child_parent.3), custom_call_target="tpu_custom_call" | custom-call | tf_op jit(solution)/shard_map/finish/pallas_call | solution.py:531
  129.3 0.0 copy-start
  129.3 5.9 %unfold.1 = f32[8,256,256]{2,1,0:T(8,128)} custom-call(f32[8,192,256]{2,1,0:T(8,128)} %finish.1.packed), custom_call_target="tpu_custom_call" | custom-call | tf_op jit(solution)/shard_map/unfold/pallas_call | solution.py:544
  135.3 0.0 copy-done
  135.3 0.8 copy.13
Async XLA Ops:
  129.3 5.9 %copy-start = (f32[2,256,256]{2,1,0:T(8,128)S(1)}, f32[2,256,256]{2,1,0:T(8,128)}, u32[]{:S(2)}) copy-start(f32[2,256,256]{2,1,0:T(8,128)} %get-tuple-element.15) | copy-start | bytes 1572868
